TPU v7x, 32 devices: a whole 2x2x4 slice. The times are simulated.
32 devices in a mesh: groups: 2 (over x), tensor: 16 (over z, y, core).
Axes of the slice: x: 2, y: 2, z: 4, core: 2. Of those that a mesh axis runs over, the one named last changes fastest.
Arguments:
- gate_act: bfloat16 [53248, 32], P('tensor', 'groups'), parts along dimension 1, may hold values from -6 to 6
- up_act: bfloat16 [53248, 32], P('tensor', 'groups'), parts along dimension 1, may hold values from -6 to 6
- codes: int32 [26624, 8192], P('tensor'), may hold values from 0 to 255
- scales: bfloat16 [1664, 8192], P('tensor'), may hold values from 0.00039863586 to 0.0015945435
Outputs:
- ffn_out: bfloat16 [32, 8192], P(('groups', 'tensor')), parts along dimension 0
There are 2 independent parts, one for each index of `groups`. A program takes and returns all parts, laid end to end along the dimension named above; an argument that names none is the same for every part. Nothing has to cross between parts.
All inputs are finite; a program needn't handle non-finite values.
Results may differ from a plain program's by a relative error of at most 0.007.
Values may be sent and summed in bfloat16 or wider, within the bound.
A program may use at most 384 MiB of HBM per device.

v0:
```python
import math

import jax
import jax.numpy as jnp
import numpy as np
from jax import lax
from jax.sharding import PartitionSpec as P

HAD_CROSS = 128
GROUP = 32
HAD_LOCAL = 416


def swapped(value, axis, distance):
    mask = 2**distance
    pairs = [(source, source ^ mask) for source in range(lax.axis_size(axis))]
    return lax.ppermute(value, axis, pairs)


def paley_table():
    squares = set()
    for real_part in range(5):
        for root_part in range(5):
            squares.add(
                (
                    (real_part * real_part + 2 * root_part * root_part) % 5,
                    2 * real_part * root_part % 5,
                )
            )
    jacobsthal = np.zeros((25, 25))
    for first in range(25):
        for second in range(25):
            differ = ((first // 5 - second // 5) % 5, (first % 5 - second % 5) % 5)
            if differ == (0, 0):
                jacobsthal[first, second] = 0.0
            elif differ in squares:
                jacobsthal[first, second] = 1.0
            else:
                jacobsthal[first, second] = -1.0
    conference = np.zeros((26, 26))
    conference[0, 1:] = 1.0
    conference[1:, 0] = 1.0
    conference[1:, 1:] = jacobsthal
    return np.kron(conference, np.array([[1.0, 1.0], [1.0, -1.0]])) + np.kron(
        np.eye(26), np.array([[1.0, -1.0], [-1.0, -1.0]])
    )


def walsh_table(order):
    matrix = np.ones((1, 1))
    while matrix.shape[0] < order:
        matrix = np.kron(np.array([[1.0, 1.0], [1.0, -1.0]]), matrix)
    return matrix


def hadamard_local(order):
    matrix = np.kron(walsh_table(order // 52), paley_table()) / math.sqrt(order)
    return jnp.asarray(matrix, dtype=jnp.float32).astype(jnp.bfloat16)


def sign_table(order):
    row_index = jnp.arange(order, dtype=jnp.int32)[:, None]
    col_index = jnp.arange(order, dtype=jnp.int32)[None, :]
    shared = jnp.zeros((order, order), jnp.int32)
    for bit_pos in range(order.bit_length() - 1):
        shared = shared + row_index // 2**bit_pos % 2 * (col_index // 2**bit_pos % 2)
    return (1 - 2 * (shared % 2)).astype(jnp.float32)


def dequantize(words, group_scales):
    low_codes = words % 16
    high_codes = words // 16
    unpacked = jnp.stack([low_codes, high_codes], axis=1).reshape(
        2 * words.shape[0], words.shape[1]
    )
    spread = jnp.repeat(group_scales.astype(jnp.float32), GROUP, axis=0)
    return ((unpacked - 8).astype(jnp.float32) * spread).astype(jnp.bfloat16)


def body(gate_act, up_act, codes, scales):
    units_here = gate_act.shape[0]
    total_rows = gate_act.shape[1]
    blocks_here = units_here // HAD_LOCAL
    factor = 1.0 / math.sqrt(HAD_CROSS)
    hidden = (jax.nn.silu(gate_act.astype(jnp.float32)) * up_act.astype(jnp.float32)).astype(
        jnp.bfloat16
    )
    hidden = hidden.reshape(blocks_here, HAD_LOCAL, total_rows)
    local_table = hadamard_local(HAD_LOCAL)
    local = jnp.einsum(
        "kn,anr->akr", local_table, hidden, preferred_element_type=jnp.float32
    ).astype(jnp.bfloat16)
    partial_sums = jnp.einsum(
        "abr,ae->ebr",
        local.astype(jnp.float32),
        sign_table(blocks_here),
        precision=lax.Precision.HIGHEST,
    )
    my_index = lax.axis_index("tensor")
    for bit_pos in range(lax.axis_size("tensor").bit_length() - 1):
        partner = swapped(partial_sums, "tensor", bit_pos)
        upper = my_index // 2**bit_pos % 2
        partial_sums = jnp.where(upper == 0, partial_sums + partner, partner - partial_sums)
    rotated = (partial_sums * factor).astype(jnp.bfloat16)
    rotated = rotated.reshape(units_here, total_rows)
    weight = dequantize(codes, scales)
    summed = lax.psum_scatter(
        lax.dot_general(
            rotated, weight, (((0,), (0,)), ((), ())), preferred_element_type=jnp.float32
        ),
        "tensor",
        scatter_dimension=0,
        tiled=True,
    )
    return summed.astype(jnp.bfloat16)


def solution(mesh):
    placed = (P("tensor", "groups"), P("tensor", "groups"), P("tensor", None), P("tensor", None))
    return jax.shard_map(
        body, mesh=mesh, in_specs=placed, out_specs=P(("groups", "tensor"), None), check_vma=False
    )
```

profile of v0, /device:TPU:0, one launch (start us, length us, event | category | flops | bytes accessed | tf_op | source)
XLA Modules:
  0.0 578.5 jit_solution(2207300311553692333)
XLA Ops:
  0.0 1.0 fusion.10
  1.0 0.2 reshape.291
  1.3 1.3 fusion.5
  2.5 0.3 fusion.16
  2.9 0.6 collective-permute-start
  3.5 1.2 collective-permute-done
  4.7 2.9 collective-permute-start.1
  7.6 53.2 %fusion.1 = (s32[1664,1,8192]{2,0,1:T(8,128)}, s32[1664,1,8192]{2,0,1:T(8,128)}) fusion(s32[1664,8192]{1,0:T(8,128)} %param.7), kind=kLoop, calls=%fused_computation.8 | loop fusion | flops 258998272 | bytes 163577856 | tf_op jit(solution)/shard_map/stack | solution.py:73
  60.8 0.0 collective-permute-done.1
  60.8 0.8 subtract_select_fusion.1
  61.5 1.6 collective-permute-start.2
  63.1 70.4 %fusion = f32[1664,2,8192]{2,0,1:T(8,128)} fusion(s32[1664,1,8192]{2,0,1:T(8,128)} %get-tuple-element.6, s32[1664,1,8192]{2,0,1:T(8,128)} %get-tuple-element.5), kind=kLoop, calls=%fused_computation.1 | loop fusion | flops 81788928 | bytes 218103808 | tf_op jit(solution)/shard_map/convert_element_type | solution.py:77
  133.5 173.9 %copy.7 = f32[1664,2,8192]{2,1,0:T(2,128)} copy(f32[1664,2,8192]{2,0,1:T(8,128)} %fusion) | data formatting | bytes 218103808 | tf_op jit(solution)/shard_map/convert_element_type | solution.py:77
  307.4 126.4 %convert_element_type.65 = f32[104,32,8192]{2,1,0:T(8,128)} reshape(f32[1664,2,8192]{2,1,0:T(2,128)} %copy.7) | data formatting | bytes 218103808 | tf_op jit(solution)/shard_map/convert_element_type | solution.py:77
  433.8 1.8 convert_element_type.66
  435.6 0.0 collective-permute-done.2
  435.6 1.8 subtract_select_fusion
  437.4 0.0 copy-start
  437.4 2.6 collective-permute-start.3
  440.0 52.2 %multiply_convert_fusion = bf16[104,32,8192]{2,1,0:T(8,128)(2,1)} fusion(f32[104,32,8192]{2,1,0:T(8,128)} %convert_element_type.65, f32[104,8192]{1,0:T(8,128)S(1)} %convert_element_type.66), kind=kLoop, calls=%fused_computation.2 | loop fusion | flops 54525952 | bytes 166985728 | tf_op jit(solution)/shard_map/convert_element_type | solution.py:77
  492.2 0.0 copy-done
  492.2 0.6 dynamic-slice
  492.8 0.0 collective-permute-done.3
  492.8 1.1 multiply_convert_fusion.1
  493.9 0.2 reshape.292
  494.1 20.3 %fusion.35 = f32[16,8192]{1,0:T(8,128)S(1)} fusion(bf16[3328,16]{0,1:T(8,128)(2,1)S(1)} %reshape.292, bf16[3328,8192]{1,0:T(8,128)(2,1)} %bitcast.21), kind=kOutput, calls=%fused_computation.67 | convolution fusion | flops 872415232 | bytes 55156736 | tf_op jit(solution)/shard_map/dot_general | solution.py:108
  514.3 62.9 %all-reduce.2 = bf16[16,8192]{1,0:T(8,128)(2,1)S(1)} all-reduce(f32[16,8192]{1,0:T(8,128)S(1)} %fusion.35), channel_id=2, replica_groups=mesh['groups'=2,'tensor'=16] {'tensor'}, use_global_device_ids=true, to_apply=%region_0.1.clone | all-reduce | flops 131072 | bytes 786432
  577.3 1.2 dynamic-slice_convert_fusion
  (3 shorter events, 0.0 us)
Async XLA Ops:
  2.9 1.7 collective-permute-start
  4.7 56.1 %collective-permute-start.1 = (f32[8,416,16]{1,0,2:T(8,128)S(1)}, f32[8,416,16]{1,0,2:T(8,128)S(1)}, u32[]{:S(2)}, u32[]{:S(2)}) collective-permute-start(f32[8,416,16]{1,0,2:T(8,128)S(1)} %subtract_select_fusion.2), channel_id=1, source_target_pairs={{0,2},{1,3},{2,0},{3,1},{4,6},{5,7},{6,4},{7,5},{8,10},{9,11},{10,... | collective-permute-start | bytes 638984 | tf_op jit(solution)/shard_map/ppermute | solution.py:17
  61.5 374.1 %collective-permute-start.2 = (f32[8,416,16]{1,0,2:T(8,128)}, f32[8,416,16]{1,0,2:T(8,128)}, u32[]{:S(2)}, u32[]{:S(2)}) collective-permute-start(f32[8,416,16]{1,0,2:T(8,128)} %subtract_select_fusion.1), channel_id=1, source_target_pairs={{0,4},{1,5},{2,6},{3,7},{4,0},{5,1},{6,2},{7,3},{8,12},{9,13},{10,... | collective-permute-start | bytes 638984 | tf_op jit(solution)/shard_map/ppermute | solution.py:17
  437.4 54.8 %copy-start = (u32[32]{0:T(128)S(1)}, u32[32]{0:T(128)}, u32[]{:S(2)}) copy-start(u32[32]{0:T(128)} %constant.212) | copy-start | bytes 388
  437.4 55.4 %collective-permute-start.3 = (f32[8,416,16]{1,0,2:T(8,128)}, f32[8,416,16]{1,0,2:T(8,128)}, u32[]{:S(2)}, u32[]{:S(2)}) collective-permute-start(f32[8,416,16]{1,0,2:T(8,128)} %subtract_select_fusion), channel_id=1, source_target_pairs={{0,8},{1,9},{2,10},{3,11},{4,12},{5,13},{6,14},{7,15},{8,0},{9,1},... | collective-permute-start | bytes 638984 | tf_op jit(solution)/shard_map/ppermute | solution.py:17
where the time goes:
time: 582 us; the launch traced here: 578 us
  local copies, waits for them, and re-layouts  302 us (52%)
  other arithmetic  182 us (31%)
  blocking collectives  62.9 us (11%)
  matrix products  21.9 us (4%)
  starting transfers between devices  7.67 us (1%)
    convert_element_type x2, local copies, waits for them, and re-layouts, dequantize(): return ((unpacked - 8).astype(jnp.float32) * spread).astype(jnp.bfloat16)  300 us
    convert_element_type x2, other arithmetic, dequantize(): return ((unpacked - 8).astype(jnp.float32) * spread).astype(jnp.bfloat16)  123 us
    unnamed x1, blocking collectives  62.9 us
    another operation x1, other arithmetic, dequantize(): jnp.stack([low_codes, high_codes], axis=1)  53.2 us
    dot_general x1, matrix products, body(): lax.dot_general(rotated, weight, (((0,), (0,)), ((), ())), preferred_elem...  20.3 us
  transfers between devices with their start and end apart: 4, of which 1 were waited for; matrix products, arithmetic and copies ran while one was open for 83% of the time, Pallas kernels for 0%

commit v1 on v0

--- a/solution.py
+++ b/solution.py
@@ -1,9 +1,12 @@
+import functools
 import math
 
 import jax
 import jax.numpy as jnp
 import numpy as np
 from jax import lax
+from jax.experimental import pallas as pl
+from jax.experimental.pallas import tpu as pltpu
 from jax.sharding import PartitionSpec as P
 
 HAD_CROSS = 128
@@ -115,8 +118,238 @@
     return summed.astype(jnp.bfloat16)
 
 
+MESH = pl.DeviceIdType.MESH
+CHUNK = 512
+PAD = 512
+
+
+def local_padded(order):
+    matrix = np.kron(walsh_table(order // 52), paley_table()) / math.sqrt(order)
+    half = order // 2
+    table = np.zeros((order, PAD), np.float32)
+    table[:, :half] = matrix[0::2].T
+    table[:, PAD // 2 : PAD // 2 + half] = matrix[1::2].T
+    return jnp.asarray(table).astype(jnp.bfloat16)
+
+
+def swap_table(outer, inner):
+    table = np.zeros((outer * inner, outer * inner), np.float32)
+    for i in range(outer):
+        for j in range(inner):
+            table[j * outer + i, i * inner + j] = 1.0
+    return jnp.asarray(table).astype(jnp.bfloat16)
+
+
+def f32_dot(left, right):
+    return jnp.dot(left, right, preferred_element_type=jnp.float32)
+
+
+def fused_kernel(
+    sizes,
+    gate_ref, up_ref, codes_ref, scales_ref, table_ref, walsh_ref, swap1_ref, swap2_ref, swap3_ref,
+    out_ref,
+    words, scale16, scale32, snd1, rcv1, snd2, rcv2, rot, acc, snd3, rcv3,
+    code_sem, scale_sem, send1, recv1, send2, recv2, send3, recv3,
+):
+    groups, ranks, blocks, chunks = sizes
+    rows = groups * ranks
+    half_words = HAD_LOCAL // 2
+    bands = HAD_LOCAL // GROUP
+    band = GROUP // 2
+    my_group = lax.axis_index("groups")
+    my_rank = lax.axis_index("tensor")
+    me = my_group * ranks + my_rank
+    base = my_group * (chunks * CHUNK)
+
+    def code_copy(j):
+        start = pl.multiple_of(base + j * CHUNK, CHUNK)
+        return pltpu.make_async_copy(
+            codes_ref.at[:, pl.ds(start, CHUNK)], words.at[j], code_sem.at[j]
+        )
+
+    scale_copy = pltpu.make_async_copy(
+        scales_ref.at[:, pl.ds(pl.multiple_of(base, CHUNK), chunks * CHUNK)], scale16, scale_sem
+    )
+    scale_copy.start()
+
+    @pl.loop(0, chunks)
+    def _(j):
+        code_copy(j).start()
+
+    barrier = pltpu.get_barrier_semaphore()
+
+    @pl.loop(1, rows)
+    def _(k):
+        peer = lax.rem(me + k, rows)
+        pl.semaphore_signal(
+            barrier, inc=1, device_id=(peer // ranks, lax.rem(peer, ranks)), device_id_type=MESH
+        )
+
+    table = table_ref[...]
+    parts = []
+    for a in range(blocks):
+        gate = gate_ref[a * HAD_LOCAL : (a + 1) * HAD_LOCAL, :].astype(jnp.float32)
+        up = up_ref[a * HAD_LOCAL : (a + 1) * HAD_LOCAL, :].astype(jnp.float32)
+        hidden = (gate / (1.0 + jnp.exp(-gate)) * up).astype(jnp.bfloat16)
+        parts.append(
+            lax.dot_general(
+                hidden, table, (((0,), (0,)), ((), ())), preferred_element_type=jnp.float32
+            ).astype(jnp.bfloat16)
+        )
+    local = f32_dot(swap1_ref[...], jnp.concatenate(parts, axis=0))
+    snd1[...] = local.reshape(ranks, blocks, PAD).astype(jnp.bfloat16)
+    rcv1[my_rank] = snd1[my_rank]
+    pl.semaphore_wait(barrier, rows - 1)
+
+    def copy1(k):
+        peer = lax.rem(my_rank + k, ranks)
+        return pltpu.make_async_remote_copy(
+            src_ref=snd1.at[peer], dst_ref=rcv1.at[my_rank],
+            send_sem=send1.at[k], recv_sem=recv1.at[k],
+            device_id=(my_group, peer), device_id_type=MESH,
+        )
+
+    @pl.loop(1, ranks)
+    def _(k):
+        copy1(k).start()
+
+    scale_copy.wait()
+    scale32[...] = scale16[...].astype(jnp.float32)
+
+    @pl.loop(1, ranks)
+    def _(k):
+        copy1(k).wait()
+
+    gathered = rcv1[...].astype(jnp.float32).reshape(ranks * blocks, PAD).astype(jnp.bfloat16)
+    rotated = f32_dot(walsh_ref[...], gathered) * (1.0 / math.sqrt(HAD_CROSS))
+    snd2[...] = rotated.reshape(ranks, blocks, PAD).astype(jnp.bfloat16)
+    rcv2[me] = snd2[my_rank]
+
+    def copy2(k):
+        peer = lax.rem(me + k, rows)
+        return pltpu.make_async_remote_copy(
+            src_ref=snd2.at[lax.rem(peer, ranks)], dst_ref=rcv2.at[me],
+            send_sem=send2.at[k], recv_sem=recv2.at[k],
+            device_id=(peer // ranks, lax.rem(peer, ranks)), device_id_type=MESH,
+        )
+
+    @pl.loop(1, rows)
+    def _(k):
+        copy2(k).start()
+
+    @pl.loop(1, rows)
+    def _(k):
+        copy2(k).wait()
+
+    gathered = rcv2[...].astype(jnp.float32).reshape(rows * blocks, PAD).astype(jnp.bfloat16)
+    rot[...] = f32_dot(swap2_ref[...], gathered).astype(jnp.bfloat16)
+
+    gap = jnp.zeros((PAD // 2 - half_words, CHUNK), jnp.bfloat16)
+
+    @pl.loop(0, chunks)
+    def _(j):
+        code_copy(j).wait()
+        columns = pl.ds(pl.multiple_of(j * CHUNK, CHUNK), CHUNK)
+        total = jnp.zeros((rows, CHUNK), jnp.float32)
+        for a in range(blocks):
+            low, high = [], []
+            for n in range(bands):
+                word = words[j, a * half_words + n * band : a * half_words + (n + 1) * band, :]
+                row = a * bands + n
+                scale = jnp.broadcast_to(scale32[row : row + 1, columns], (band, CHUNK)).astype(
+                    jnp.bfloat16
+                )
+                low.append(((word & 15).astype(jnp.float32).astype(jnp.bfloat16) - 8) * scale)
+                high.append(((word >> 4).astype(jnp.float32).astype(jnp.bfloat16) - 8) * scale)
+            weight = jnp.concatenate(low + [gap] + high + [gap], axis=0)
+            total = total + f32_dot(rot[a * rows : (a + 1) * rows, :], weight)
+        acc[pl.ds(pl.multiple_of(j * rows, rows), rows), :] = total.astype(jnp.bfloat16)
+
+    sums = f32_dot(swap3_ref[...], acc[...])
+    snd3[...] = sums.reshape(rows, chunks, CHUNK).astype(jnp.bfloat16)
+    rcv3[me] = snd3[me]
+
+    def copy3(k):
+        peer = lax.rem(me + k, rows)
+        return pltpu.make_async_remote_copy(
+            src_ref=snd3.at[peer], dst_ref=rcv3.at[me],
+            send_sem=send3.at[k], recv_sem=recv3.at[k],
+            device_id=(peer // ranks, lax.rem(peer, ranks)), device_id_type=MESH,
+        )
+
+    @pl.loop(1, rows)
+    def _(k):
+        copy3(k).start()
+
+    @pl.loop(1, rows)
+    def _(k):
+        copy3(k).wait()
+
+    for g in range(groups):
+        out_ref[g] = jnp.sum(rcv3[g * ranks : (g + 1) * ranks].astype(jnp.float32), axis=0).astype(
+            jnp.bfloat16
+        )
+
+
+def fused_body(gate_act, up_act, codes, scales):
+    groups, ranks = lax.axis_size("groups"), lax.axis_size("tensor")
+    rows = groups * ranks
+    blocks = gate_act.shape[0] // HAD_LOCAL
+    width = codes.shape[1]
+    chunks = width // groups // CHUNK
+    vmem = pl.BlockSpec(memory_space=pltpu.VMEM)
+    hbm = pl.BlockSpec(memory_space=pl.ANY)
+    bf16 = jnp.bfloat16
+    walsh = jnp.asarray(walsh_table(HAD_CROSS), jnp.float32).astype(bf16)
+    out = pl.pallas_call(
+        functools.partial(fused_kernel, (groups, ranks, blocks, chunks)),
+        out_shape=jax.ShapeDtypeStruct((groups, chunks, CHUNK), bf16),
+        in_specs=[vmem, vmem, hbm, hbm] + [vmem] * 5,
+        out_specs=vmem,
+        scratch_shapes=[
+            pltpu.VMEM((chunks, codes.shape[0], CHUNK), jnp.int32),
+            pltpu.VMEM((scales.shape[0], chunks * CHUNK), bf16),
+            pltpu.VMEM((scales.shape[0], chunks * CHUNK), jnp.float32),
+            pltpu.VMEM((ranks, blocks, PAD), bf16),
+            pltpu.VMEM((ranks, blocks, PAD), bf16),
+            pltpu.VMEM((ranks, blocks, PAD), bf16),
+            pltpu.VMEM((rows, blocks, PAD), bf16),
+            pltpu.VMEM((blocks * rows, PAD), bf16),
+            pltpu.VMEM((chunks * rows, CHUNK), bf16),
+            pltpu.VMEM((rows, chunks, CHUNK), bf16),
+            pltpu.VMEM((rows, chunks, CHUNK), bf16),
+            pltpu.SemaphoreType.DMA((chunks,)),
+            pltpu.SemaphoreType.DMA,
+            pltpu.SemaphoreType.DMA((ranks,)),
+            pltpu.SemaphoreType.DMA((ranks,)),
+            pltpu.SemaphoreType.DMA((rows,)),
+            pltpu.SemaphoreType.DMA((rows,)),
+            pltpu.SemaphoreType.DMA((rows,)),
+            pltpu.SemaphoreType.DMA((rows,)),
+        ],
+        compiler_params=pltpu.CompilerParams(
+            collective_id=0, has_side_effects=True, vmem_limit_bytes=60 * 1024 * 1024
+        ),
+    )(
+        gate_act, up_act, codes, scales,
+        local_padded(HAD_LOCAL), walsh,
+        swap_table(blocks, ranks), swap_table(rows, blocks), swap_table(chunks, rows),
+    )
+    return out.reshape(1, width)
+
+
+def choose(gate_act, up_act, codes, scales):
+    groups, ranks = lax.axis_size("groups"), lax.axis_size("tensor")
+    fused = (
+        gate_act.shape[0] // HAD_LOCAL % 8 == 0
+        and gate_act.shape[1] == ranks
+        and codes.shape[1] % (groups * CHUNK * 8) == 0
+    )
+    return (fused_body if fused else body)(gate_act, up_act, codes, scales)
+
+
 def solution(mesh):
     placed = (P("tensor", "groups"), P("tensor", "groups"), P("tensor", None), P("tensor", None))
     return jax.shard_map(
-        body, mesh=mesh, in_specs=placed, out_specs=P(("groups", "tensor"), None), check_vma=False
-    )
+        choose, mesh=mesh, in_specs=placed, out_specs=P(("groups", "tensor"), None), check_vma=False
+    )

time: 582 us -> 45.7 us (0.08)
  local copies, waits for them, and re-layouts: 302 us -> 5.59 us
  other arithmetic: 182 us -> 0 us
  blocking collectives: 62.9 us -> 0 us
  Pallas kernels: 0 us -> 39.9 us
  matrix products: 21.9 us -> 0 us
  starting transfers between devices: 7.67 us -> 0 us
    convert_element_type x3 -> x0, local copies, waits for them, and re-layouts: 302 us -> none  [the longest x2 300 us: dequantize(): return ((unpacked - 8).astype(jnp.float32) * spread).astype(jnp.bfloat16)]
    convert_element_type x5 -> x0, other arithmetic: 126 us -> none  [the longest x2 123 us: dequantize(): return ((unpacked - 8).astype(jnp.float32) * spread).astype(jnp.bfloat16)]
    unnamed x1 -> x0, blocking collectives: 62.9 us -> none
    another operation x1 -> x0, other arithmetic: 53.2 us -> none  [dequantize(): jnp.stack([low_codes, high_codes], axis=1)]
    pallas_call x0 -> x1, Pallas kernels: none -> 39.9 us  [fused_body(): pl.pallas_call(functools.partial(fused_kernel, (groups, ranks, blocks, ch...]
    dot_general x3 -> x0, matrix products: 21.9 us -> none  [the longest x1 20.3 us: body(): lax.dot_general(rotated, weight, (((0,), (0,)), ((), ())), preferred_elem...]
    ppermute x4 -> x0, starting transfers between devices: 7.67 us -> none  [swapped(): return lax.ppermute(value, axis, pairs)]
  transfers between devices with their start and end apart: 4 -> 0, of which waited for: 1 -> 0; matrix products, arithmetic and copies ran while one was open for 83% -> 0% of each run, Pallas kernels for 0% -> 0%
where the time goes in v1:
time: 45.7 us; the launch traced here: 45.5 us
  Pallas kernels  39.9 us (87%)
  local copies, waits for them, and re-layouts  5.59 us (12%)
    pallas_call x1, Pallas kernels, fused_body(): pl.pallas_call(functools.partial(fused_kernel, (groups, ranks, blocks, ch...  39.9 us
    unnamed x2, local copies, waits for them, and re-layouts  4.24 us
    reshape x1, local copies, waits for them, and re-layouts, fused_body(): return out.reshape(1, width)  1.35 us

profile of v1, /device:TPU:0, one launch (start us, length us, event | category | flops | bytes accessed | tf_op | source)
XLA Modules:
  0.0 45.5 jit_solution(17333045001651454524)
XLA Ops:
  0.0 2.1 %copy.10.gate_ref = bf16[3328,16]{1,0:T(8,128)(2,1)} copy(bf16[3328,16]{0,1:T(8,128)(2,1)} %param.9) | data formatting | bytes 212992 | tf_op args[0]
  2.1 2.1 %copy.11.up_ref = bf16[3328,16]{1,0:T(8,128)(2,1)} copy(bf16[3328,16]{0,1:T(8,128)(2,1)} %param.10) | data formatting | bytes 212992 | tf_op args[1]
  4.2 39.9 %shard_map.91 = bf16[2,8,512]{2,1,0:T(8,128)(2,1)} custom-call(bf16[3328,16]{1,0:T(8,128)(2,1)} %copy.10.gate_ref, bf16[3328,16]{1,0:T(8,128)(2,1)} %copy.11.up_ref, s32[1664,8192]{1,0:T(8,128)} %codes_ref.1, bf16[104,8192]{1,0:T(8,128)(2,1)} %scales_ref.1, bf16[416,512]{1,0:T(8,128)(2,1)} %constant.16.table_ref, bf16[128,128]{1,0:T(8,128)(2,1)} %constant.17.walsh_ref, ...), custom_call_target="tpu_custom_call" | custom-call | tf_op jit(solution)/shard_map/pallas_call | solution.py:304
  44.1 1.3 %reshape.3 = bf16[1,8192]{1,0:T(2,128)(2,1)} reshape(bf16[2,8,512]{2,1,0:T(8,128)(2,1)} %shard_map.91) | data formatting | bytes 32768 | tf_op jit(solution)/shard_map/reshape | solution.py:338

commit v2 on v1

--- a/solution.py
+++ b/solution.py
@@ -121,6 +121,8 @@
 MESH = pl.DeviceIdType.MESH
 CHUNK = 512
 PAD = 512
+PARTS = 2
+SPLITS = (2, 5)
 
 
 def local_padded(order):
@@ -128,7 +130,7 @@
     half = order // 2
     table = np.zeros((order, PAD), np.float32)
     table[:, :half] = matrix[0::2].T
-    table[:, PAD // 2 : PAD // 2 + half] = matrix[1::2].T
+    table[:, half : 2 * half] = matrix[1::2].T
     return jnp.asarray(table).astype(jnp.bfloat16)
 
 
@@ -148,7 +150,7 @@
     sizes,
     gate_ref, up_ref, codes_ref, scales_ref, table_ref, walsh_ref, swap1_ref, swap2_ref, swap3_ref,
     out_ref,
-    words, scale16, scale32, snd1, rcv1, snd2, rcv2, rot, acc, snd3, rcv3,
+    words, weights, scale16, scale32, snd1, rcv1, snd2, rcv2, rot, acc, snd3, rcv3,
     code_sem, scale_sem, send1, recv1, send2, recv2, send3, recv3,
 ):
     groups, ranks, blocks, chunks = sizes
@@ -185,20 +187,39 @@
             barrier, inc=1, device_id=(peer // ranks, lax.rem(peer, ranks)), device_id_type=MESH
         )
 
-    table = table_ref[...]
-    parts = []
-    for a in range(blocks):
-        gate = gate_ref[a * HAD_LOCAL : (a + 1) * HAD_LOCAL, :].astype(jnp.float32)
-        up = up_ref[a * HAD_LOCAL : (a + 1) * HAD_LOCAL, :].astype(jnp.float32)
-        hidden = (gate / (1.0 + jnp.exp(-gate)) * up).astype(jnp.bfloat16)
-        parts.append(
-            lax.dot_general(
-                hidden, table, (((0,), (0,)), ((), ())), preferred_element_type=jnp.float32
-            ).astype(jnp.bfloat16)
-        )
+    def dequantize_chunk(j):
+        code_copy(j).wait()
+        columns = pl.ds(pl.multiple_of(j * CHUNK, CHUNK), CHUNK)
+        for a in range(blocks):
+            for n in range(bands):
+                word = words[j, a * half_words + n * band : a * half_words + (n + 1) * band, :]
+                row = a * bands + n
+                scale = jnp.broadcast_to(scale32[row : row + 1, columns], (band, CHUNK)).astype(
+                    jnp.bfloat16
+                )
+                low = ((word & 15).astype(jnp.float32).astype(jnp.bfloat16) - 8) * scale
+                high = ((word >> 4).astype(jnp.float32).astype(jnp.bfloat16) - 8) * scale
+                at = a * HAD_LOCAL + n * band
+                weights[j, at : at + band, :] = low
+                weights[j, at + half_words : at + half_words + band, :] = high
+
+    def dequantize_chunks(first, last):
+        @pl.loop(first, last)
+        def _(j):
+            dequantize_chunk(j)
+
+    gate = gate_ref[...].astype(jnp.float32)
+    hidden = (gate / (1.0 + jnp.exp(-gate)) * up_ref[...].astype(jnp.float32)).astype(jnp.bfloat16)
+    stacked = jnp.concatenate(
+        [hidden[:, a * HAD_LOCAL : (a + 1) * HAD_LOCAL] for a in range(blocks)], axis=0
+    )
+    parts = [f32_dot(stacked, table_ref[...]).astype(jnp.bfloat16)]
     local = f32_dot(swap1_ref[...], jnp.concatenate(parts, axis=0))
     snd1[...] = local.reshape(ranks, blocks, PAD).astype(jnp.bfloat16)
     rcv1[my_rank] = snd1[my_rank]
+    scale_copy.wait()
+    scale32[...] = scale16[...].astype(jnp.float32)
+    dequantize_chunks(0, SPLITS[0])
     pl.semaphore_wait(barrier, rows - 1)
 
     def copy1(k):
@@ -213,8 +234,7 @@
     def _(k):
         copy1(k).start()
 
-    scale_copy.wait()
-    scale32[...] = scale16[...].astype(jnp.float32)
+    dequantize_chunks(SPLITS[0], SPLITS[1])
 
     @pl.loop(1, ranks)
     def _(k):
@@ -237,58 +257,53 @@
     def _(k):
         copy2(k).start()
 
+    dequantize_chunks(SPLITS[1], chunks)
+
     @pl.loop(1, rows)
     def _(k):
         copy2(k).wait()
 
     gathered = rcv2[...].astype(jnp.float32).reshape(rows * blocks, PAD).astype(jnp.bfloat16)
-    rot[...] = f32_dot(swap2_ref[...], gathered).astype(jnp.bfloat16)
-
-    gap = jnp.zeros((PAD // 2 - half_words, CHUNK), jnp.bfloat16)
-
-    @pl.loop(0, chunks)
-    def _(j):
-        code_copy(j).wait()
-        columns = pl.ds(pl.multiple_of(j * CHUNK, CHUNK), CHUNK)
-        total = jnp.zeros((rows, CHUNK), jnp.float32)
-        for a in range(blocks):
-            low, high = [], []
-            for n in range(bands):
-                word = words[j, a * half_words + n * band : a * half_words + (n + 1) * band, :]
-                row = a * bands + n
-                scale = jnp.broadcast_to(scale32[row : row + 1, columns], (band, CHUNK)).astype(
-                    jnp.bfloat16
-                )
-                low.append(((word & 15).astype(jnp.float32).astype(jnp.bfloat16) - 8) * scale)
-                high.append(((word >> 4).astype(jnp.float32).astype(jnp.bfloat16) - 8) * scale)
-            weight = jnp.concatenate(low + [gap] + high + [gap], axis=0)
-            total = total + f32_dot(rot[a * rows : (a + 1) * rows, :], weight)
-        acc[pl.ds(pl.multiple_of(j * rows, rows), rows), :] = total.astype(jnp.bfloat16)
-
-    sums = f32_dot(swap3_ref[...], acc[...])
-    snd3[...] = sums.reshape(rows, chunks, CHUNK).astype(jnp.bfloat16)
-    rcv3[me] = snd3[me]
-
-    def copy3(k):
+    ordered = f32_dot(swap2_ref[...], gathered).astype(jnp.bfloat16)
+    rot[...] = jnp.concatenate(
+        [ordered[a * rows : (a + 1) * rows, :HAD_LOCAL] for a in range(blocks)], axis=1
+    )
+
+    def copy3(part, k):
         peer = lax.rem(me + k, rows)
         return pltpu.make_async_remote_copy(
-            src_ref=snd3.at[peer], dst_ref=rcv3.at[me],
-            send_sem=send3.at[k], recv_sem=recv3.at[k],
+            src_ref=snd3.at[part, peer], dst_ref=rcv3.at[part, me],
+            send_sem=send3.at[part, k], recv_sem=recv3.at[part, k],
             device_id=(peer // ranks, lax.rem(peer, ranks)), device_id_type=MESH,
         )
 
-    @pl.loop(1, rows)
-    def _(k):
-        copy3(k).start()
-
-    @pl.loop(1, rows)
-    def _(k):
-        copy3(k).wait()
-
-    for g in range(groups):
-        out_ref[g] = jnp.sum(rcv3[g * ranks : (g + 1) * ranks].astype(jnp.float32), axis=0).astype(
-            jnp.bfloat16
-        )
+    fold = chunks // PARTS
+    width = fold * CHUNK // 8
+    for part in range(PARTS):
+        @pl.loop(0, fold)
+        def _(j):
+            total = f32_dot(rot[...], weights[part * fold + j]).astype(jnp.bfloat16)
+            for n in range(CHUNK // width):
+                at = pl.multiple_of((j * (CHUNK // width) + n) * rows, rows)
+                acc[pl.ds(at, rows), :] = total[:, n * width : (n + 1) * width]
+
+        sums = f32_dot(swap3_ref[...], acc[...])
+        snd3[part] = sums.reshape(rows, 8, width).astype(jnp.bfloat16)
+        rcv3[part, me] = snd3[part, me]
+
+        @pl.loop(1, rows)
+        def _(k):
+            copy3(part, k).start()
+
+    for part in range(PARTS):
+        @pl.loop(1, rows)
+        def _(k):
+            copy3(part, k).wait()
+
+        for g in range(groups):
+            out_ref[g, part] = jnp.sum(
+                rcv3[part, g * ranks : (g + 1) * ranks].astype(jnp.float32), axis=0
+            ).astype(jnp.bfloat16)
 
 
 def fused_body(gate_act, up_act, codes, scales):
@@ -297,43 +312,45 @@
     blocks = gate_act.shape[0] // HAD_LOCAL
     width = codes.shape[1]
     chunks = width // groups // CHUNK
+    part_width = width // groups // PARTS // 8
     vmem = pl.BlockSpec(memory_space=pltpu.VMEM)
     hbm = pl.BlockSpec(memory_space=pl.ANY)
     bf16 = jnp.bfloat16
     walsh = jnp.asarray(walsh_table(HAD_CROSS), jnp.float32).astype(bf16)
     out = pl.pallas_call(
         functools.partial(fused_kernel, (groups, ranks, blocks, chunks)),
-        out_shape=jax.ShapeDtypeStruct((groups, chunks, CHUNK), bf16),
+        out_shape=jax.ShapeDtypeStruct((groups, PARTS, 8, part_width), bf16),
         in_specs=[vmem, vmem, hbm, hbm] + [vmem] * 5,
         out_specs=vmem,
         scratch_shapes=[
             pltpu.VMEM((chunks, codes.shape[0], CHUNK), jnp.int32),
+            pltpu.VMEM((chunks, 2 * codes.shape[0], CHUNK), bf16),
             pltpu.VMEM((scales.shape[0], chunks * CHUNK), bf16),
             pltpu.VMEM((scales.shape[0], chunks * CHUNK), jnp.float32),
             pltpu.VMEM((ranks, blocks, PAD), bf16),
             pltpu.VMEM((ranks, blocks, PAD), bf16),
             pltpu.VMEM((ranks, blocks, PAD), bf16),
             pltpu.VMEM((rows, blocks, PAD), bf16),
-            pltpu.VMEM((blocks * rows, PAD), bf16),
-            pltpu.VMEM((chunks * rows, CHUNK), bf16),
-            pltpu.VMEM((rows, chunks, CHUNK), bf16),
-            pltpu.VMEM((rows, chunks, CHUNK), bf16),
+            pltpu.VMEM((rows, 2 * codes.shape[0]), bf16),
+            pltpu.VMEM((8 * rows, part_width), bf16),
+            pltpu.VMEM((PARTS, rows, 8, part_width), bf16),
+            pltpu.VMEM((PARTS, rows, 8, part_width), bf16),
             pltpu.SemaphoreType.DMA((chunks,)),
             pltpu.SemaphoreType.DMA,
             pltpu.SemaphoreType.DMA((ranks,)),
             pltpu.SemaphoreType.DMA((ranks,)),
             pltpu.SemaphoreType.DMA((rows,)),
             pltpu.SemaphoreType.DMA((rows,)),
-            pltpu.SemaphoreType.DMA((rows,)),
-            pltpu.SemaphoreType.DMA((rows,)),
+            pltpu.SemaphoreType.DMA((PARTS, rows)),
+            pltpu.SemaphoreType.DMA((PARTS, rows)),
         ],
         compiler_params=pltpu.CompilerParams(
-            collective_id=0, has_side_effects=True, vmem_limit_bytes=60 * 1024 * 1024
+            collective_id=0, has_side_effects=True, vmem_limit_bytes=67043328
         ),
     )(
-        gate_act, up_act, codes, scales,
+        gate_act.T, up_act.T, codes, scales,
         local_padded(HAD_LOCAL), walsh,
-        swap_table(blocks, ranks), swap_table(rows, blocks), swap_table(chunks, rows),
+        swap_table(blocks, ranks), swap_table(rows, blocks), swap_table(8, rows),
     )
     return out.reshape(1, width)
 

time: 45.7 us -> 39 us (0.85)
  local copies, waits for them, and re-layouts: 5.59 us -> 1.34 us
  Pallas kernels: 39.9 us -> 37.4 us
    unnamed x2 -> x0, local copies, waits for them, and re-layouts: 4.24 us -> none
    pallas_call x1, Pallas kernels: 39.9 us -> 37.4 us  [fused_body(): pl.pallas_call(functools.partial(fused_kernel, (groups, ranks, blocks, ch...]
where the time goes in v2:
time: 39 us; the launch traced here: 38.8 us
  Pallas kernels  37.4 us (96%)
  local copies, waits for them, and re-layouts  1.34 us (3%)
    pallas_call x1, Pallas kernels, fused_body(): pl.pallas_call(functools.partial(fused_kernel, (groups, ranks, blocks, ch...  37.4 us
    reshape x1, local copies, waits for them, and re-layouts, fused_body(): return out.reshape(1, width)  1.34 us

profile of v2, /device:TPU:0, one launch (start us, length us, event | category | flops | bytes accessed | tf_op | source)
XLA Modules:
  0.0 38.8 jit_solution(14376413271821312617)
XLA Ops:
  0.0 37.4 %shard_map.91 = bf16[2,2,8,256]{3,2,1,0:T(8,128)(2,1)} custom-call(bf16[16,3328]{1,0:T(8,128)(2,1)} %bitcast.4, bf16[16,3328]{1,0:T(8,128)(2,1)} %bitcast.5, s32[1664,8192]{1,0:T(8,128)} %codes_ref.1, bf16[104,8192]{1,0:T(8,128)(2,1)} %scales_ref.1, bf16[416,512]{1,0:T(8,128)(2,1)} %constant.16.table_ref, bf16[128,128]{1,0:T(8,128)(2,1)} %constant.17.walsh_ref, ...), custom_call_target="tpu_custom_call" | custom-call | tf_op jit(solution)/shard_map/pallas_call | solution.py:320
  37.4 1.3 %reshape.3 = bf16[1,8192]{1,0:T(2,128)(2,1)} reshape(bf16[2,2,8,256]{3,2,1,0:T(8,128)(2,1)} %shard_map.91) | data formatting | bytes 32768 | tf_op jit(solution)/shard_map/reshape | solution.py:355

commit v3 on v2

--- a/solution.py
+++ b/solution.py
@@ -122,7 +122,7 @@
 CHUNK = 512
 PAD = 512
 PARTS = 2
-SPLITS = (2, 5)
+SPLITS = (2, 4, 6)
 
 
 def local_padded(order):
@@ -142,6 +142,15 @@
     return jnp.asarray(table).astype(jnp.bfloat16)
 
 
+def owner_table(pieces, rows):
+    table = np.zeros((pieces * rows, pieces * rows), np.float32)
+    for piece in range(pieces):
+        for row in range(rows):
+            place = row % 2 * (rows // 2) + row // 2
+            table[place * pieces + piece, piece * rows + row] = 1.0
+    return jnp.asarray(table).astype(jnp.bfloat16)
+
+
 def f32_dot(left, right):
     return jnp.dot(left, right, preferred_element_type=jnp.float32)
 
@@ -150,8 +159,8 @@
     sizes,
     gate_ref, up_ref, codes_ref, scales_ref, table_ref, walsh_ref, swap1_ref, swap2_ref, swap3_ref,
     out_ref,
-    words, weights, scale16, scale32, snd1, rcv1, snd2, rcv2, rot, acc, snd3, rcv3,
-    code_sem, scale_sem, send1, recv1, send2, recv2, send3, recv3,
+    words, weights, scale16, scale32, snd1, rcv1, snd2, rcv2, rot, acc, snd3, half3, sum3, rcv3,
+    code_sem, scale_sem, send1, recv1, send2, recv2, send3, recv3, send4, recv4, send5, recv5,
 ):
     groups, ranks, blocks, chunks = sizes
     rows = groups * ranks
@@ -246,22 +255,42 @@
     rcv2[me] = snd2[my_rank]
 
     def copy2(k):
-        peer = lax.rem(me + k, rows)
+        peer = lax.rem(my_rank + k, ranks)
         return pltpu.make_async_remote_copy(
-            src_ref=snd2.at[lax.rem(peer, ranks)], dst_ref=rcv2.at[me],
+            src_ref=snd2.at[peer], dst_ref=rcv2.at[me],
             send_sem=send2.at[k], recv_sem=recv2.at[k],
-            device_id=(peer // ranks, lax.rem(peer, ranks)), device_id_type=MESH,
-        )
-
-    @pl.loop(1, rows)
+            device_id=(my_group, peer), device_id_type=MESH,
+        )
+
+    def forward(k):
+        slot = my_group * ranks + lax.rem(my_rank + ranks - k, ranks)
+        return pltpu.make_async_remote_copy(
+            src_ref=rcv2.at[slot], dst_ref=rcv2.at[slot],
+            send_sem=send4.at[k], recv_sem=recv4.at[k],
+            device_id=(1 - my_group, my_rank), device_id_type=MESH,
+        )
+
+    @pl.loop(1, ranks)
     def _(k):
         copy2(k).start()
 
-    dequantize_chunks(SPLITS[1], chunks)
-
-    @pl.loop(1, rows)
-    def _(k):
-        copy2(k).wait()
+    forward(0).start()
+    dequantize_chunks(SPLITS[1], SPLITS[2])
+
+    @pl.loop(1, ranks)
+    def _(k):
+        copy2(k).wait_recv()
+        forward(k).start()
+
+    dequantize_chunks(SPLITS[2], chunks)
+
+    @pl.loop(1, ranks)
+    def _(k):
+        copy2(k).wait_send()
+
+    @pl.loop(0, ranks)
+    def _(k):
+        forward(k).wait()
 
     gathered = rcv2[...].astype(jnp.float32).reshape(rows * blocks, PAD).astype(jnp.bfloat16)
     ordered = f32_dot(swap2_ref[...], gathered).astype(jnp.bfloat16)
@@ -269,41 +298,65 @@
         [ordered[a * rows : (a + 1) * rows, :HAD_LOCAL] for a in range(blocks)], axis=1
     )
 
+    cores = 2
+    my_core = lax.rem(my_rank, cores)
+    kin = rows // cores
+    spots = ranks // cores
+    my_spot = my_group * spots + my_rank // cores
+
+    def pair(part):
+        return pltpu.make_async_remote_copy(
+            src_ref=snd3.at[part, 1 - my_core], dst_ref=half3.at[part],
+            send_sem=send5.at[part], recv_sem=recv5.at[part],
+            device_id=(my_group, my_rank + 1 - 2 * my_core), device_id_type=MESH,
+        )
+
     def copy3(part, k):
-        peer = lax.rem(me + k, rows)
+        peer = lax.rem(my_spot + k, kin)
         return pltpu.make_async_remote_copy(
-            src_ref=snd3.at[part, peer], dst_ref=rcv3.at[part, me],
+            src_ref=sum3.at[part, peer], dst_ref=rcv3.at[part, my_spot],
             send_sem=send3.at[part, k], recv_sem=recv3.at[part, k],
-            device_id=(peer // ranks, lax.rem(peer, ranks)), device_id_type=MESH,
+            device_id=(peer // spots, lax.rem(peer, spots) * cores + my_core),
+            device_id_type=MESH,
         )
 
     fold = chunks // PARTS
     width = fold * CHUNK // 8
+    for part in range(PARTS + 1):
+        if part < PARTS:
+            @pl.loop(0, fold)
+            def _(j):
+                total = f32_dot(rot[...], weights[part * fold + j]).astype(jnp.bfloat16)
+                for n in range(CHUNK // width):
+                    at = pl.multiple_of((j * (CHUNK // width) + n) * rows, rows)
+                    acc[pl.ds(at, rows), :] = total[:, n * width : (n + 1) * width]
+
+            sums = f32_dot(swap3_ref[...], acc[...])
+            snd3[part] = sums.reshape(cores, kin, 8, width).astype(jnp.bfloat16)
+            pair(part).start()
+        if part > 0:
+            pair(part - 1).wait()
+            sum3[part - 1] = (
+                snd3[part - 1, my_core].astype(jnp.float32) + half3[part - 1].astype(jnp.float32)
+            ).astype(jnp.bfloat16)
+            rcv3[part - 1, my_spot] = sum3[part - 1, my_spot]
+
+            @pl.loop(1, kin)
+            def _(k):
+                copy3(part - 1, k).start()
+
     for part in range(PARTS):
-        @pl.loop(0, fold)
-        def _(j):
-            total = f32_dot(rot[...], weights[part * fold + j]).astype(jnp.bfloat16)
-            for n in range(CHUNK // width):
-                at = pl.multiple_of((j * (CHUNK // width) + n) * rows, rows)
-                acc[pl.ds(at, rows), :] = total[:, n * width : (n + 1) * width]
-
-        sums = f32_dot(swap3_ref[...], acc[...])
-        snd3[part] = sums.reshape(rows, 8, width).astype(jnp.bfloat16)
-        rcv3[part, me] = snd3[part, me]
-
-        @pl.loop(1, rows)
-        def _(k):
-            copy3(part, k).start()
-
-    for part in range(PARTS):
-        @pl.loop(1, rows)
+        @pl.loop(1, kin)
         def _(k):
             copy3(part, k).wait()
 
         for g in range(groups):
-            out_ref[g, part] = jnp.sum(
-                rcv3[part, g * ranks : (g + 1) * ranks].astype(jnp.float32), axis=0
+            total = jnp.sum(
+                rcv3[part, g * spots : (g + 1) * spots].astype(jnp.float32), axis=0
             ).astype(jnp.bfloat16)
+            for n in range(8):
+                at = ((g * PARTS + part) * 8 + n) * width
+                out_ref[:, at : at + width] = total[n : n + 1]
 
 
 def fused_body(gate_act, up_act, codes, scales):
@@ -319,7 +372,7 @@
     walsh = jnp.asarray(walsh_table(HAD_CROSS), jnp.float32).astype(bf16)
     out = pl.pallas_call(
         functools.partial(fused_kernel, (groups, ranks, blocks, chunks)),
-        out_shape=jax.ShapeDtypeStruct((groups, PARTS, 8, part_width), bf16),
+        out_shape=jax.ShapeDtypeStruct((1, width), bf16),
         in_specs=[vmem, vmem, hbm, hbm] + [vmem] * 5,
         out_specs=vmem,
         scratch_shapes=[
@@ -333,16 +386,22 @@
             pltpu.VMEM((rows, blocks, PAD), bf16),
             pltpu.VMEM((rows, 2 * codes.shape[0]), bf16),
             pltpu.VMEM((8 * rows, part_width), bf16),
-            pltpu.VMEM((PARTS, rows, 8, part_width), bf16),
-            pltpu.VMEM((PARTS, rows, 8, part_width), bf16),
+            pltpu.VMEM((PARTS, 2, rows // 2, 8, part_width), bf16),
+            pltpu.VMEM((PARTS, rows // 2, 8, part_width), bf16),
+            pltpu.VMEM((PARTS, rows // 2, 8, part_width), bf16),
+            pltpu.VMEM((PARTS, rows // 2, 8, part_width), bf16),
             pltpu.SemaphoreType.DMA((chunks,)),
             pltpu.SemaphoreType.DMA,
             pltpu.SemaphoreType.DMA((ranks,)),
             pltpu.SemaphoreType.DMA((ranks,)),
-            pltpu.SemaphoreType.DMA((rows,)),
-            pltpu.SemaphoreType.DMA((rows,)),
-            pltpu.SemaphoreType.DMA((PARTS, rows)),
-            pltpu.SemaphoreType.DMA((PARTS, rows)),
+            pltpu.SemaphoreType.DMA((ranks,)),
+            pltpu.SemaphoreType.DMA((ranks,)),
+            pltpu.SemaphoreType.DMA((PARTS, rows // 2)),
+            pltpu.SemaphoreType.DMA((PARTS, rows // 2)),
+            pltpu.SemaphoreType.DMA((ranks,)),
+            pltpu.SemaphoreType.DMA((ranks,)),
+            pltpu.SemaphoreType.DMA((PARTS,)),
+            pltpu.SemaphoreType.DMA((PARTS,)),
         ],
         compiler_params=pltpu.CompilerParams(
             collective_id=0, has_side_effects=True, vmem_limit_bytes=67043328
@@ -350,9 +409,9 @@
     )(
         gate_act.T, up_act.T, codes, scales,
         local_padded(HAD_LOCAL), walsh,
-        swap_table(blocks, ranks), swap_table(rows, blocks), swap_table(8, rows),
-    )
-    return out.reshape(1, width)
+        swap_table(blocks, ranks), swap_table(rows, blocks), owner_table(8, rows),
+    )
+    return out
 
 
 def choose(gate_act, up_act, codes, scales):
@@ -360,6 +419,8 @@
     fused = (
         gate_act.shape[0] // HAD_LOCAL % 8 == 0
         and gate_act.shape[1] == ranks
+        and groups == 2
+        and ranks % 2 == 0
         and codes.shape[1] % (groups * CHUNK * 8) == 0
     )
     return (fused_body if fused else body)(gate_act, up_act, codes, scales)

time: 39 us -> 38 us (0.974)
  Pallas kernels: 37.4 us -> 36.4 us
    unnamed x0 -> x1, local copies, waits for them, and re-layouts: none -> 1.41 us
    reshape x1 -> x0, local copies, waits for them, and re-layouts: 1.34 us -> none  [fused_body(): return out.reshape(1, width)]
    pallas_call x1, Pallas kernels: 37.4 us -> 36.4 us  [fused_body(): pl.pallas_call(functools.partial(fused_kernel, (groups, ranks, blocks, ch...]
where the time goes in v3:
time: 38 us; the launch traced here: 37.8 us
  Pallas kernels  36.4 us (96%)
  local copies, waits for them, and re-layouts  1.41 us (4%)
    pallas_call x1, Pallas kernels, fused_body(): pl.pallas_call(functools.partial(fused_kernel, (groups, ranks, blocks, ch...  36.4 us
    unnamed x1, local copies, waits for them, and re-layouts  1.41 us

profile of v3, /device:TPU:0, one launch (start us, length us, event | category | flops | bytes accessed | tf_op | source)
XLA Modules:
  0.0 37.8 jit_solution(4569910049653336707)
XLA Ops:
  0.0 36.4 %shard_map.91 = bf16[1,8192]{1,0:T(2,128)(2,1)} custom-call(bf16[16,3328]{1,0:T(8,128)(2,1)} %bitcast.2, bf16[16,3328]{1,0:T(8,128)(2,1)} %bitcast.3, s32[1664,8192]{1,0:T(8,128)} %codes_ref.1, bf16[104,8192]{1,0:T(8,128)(2,1)} %scales_ref.1, bf16[416,512]{1,0:T(8,128)(2,1)} %constant.16.table_ref, bf16[128,128]{1,0:T(8,128)(2,1)} %constant.17.walsh_ref, ...), custom_call_target="tpu_custom_call" | custom-call | tf_op jit(solution)/shard_map/pallas_call | solution.py:373
  36.4 1.4 %copy.11 = bf16[1,8192]{1,0:T(2,128)(2,1)} copy(bf16[1,8192]{1,0:T(2,128)(2,1)} %shard_map.91) | data formatting | bytes 32768
